TPU v7x, 32 devices: a whole 2x2x4 slice. The times are simulated.
32 devices in a mesh: groups: 2 (over x), ctx: 16 (over z, y, core).
Axes of the slice: x: 2, y: 2, z: 4, core: 2. Of those that a mesh axis runs over, the one named last changes fastest.
Arguments:
- query: bfloat16 [4096, 1536], P(('groups', 'ctx')), parts along dimension 0, may hold values from -5 to 5
- key_rows: bfloat16 [4096, 1536], P(('groups', 'ctx')), parts along dimension 0, may hold values from -5 to 5
- value: bfloat16 [4096, 1536], P(('groups', 'ctx')), parts along dimension 0, may hold values from -6 to 6
- grad_out: bfloat16 [4096, 1536], P(('groups', 'ctx')), parts along dimension 0, may hold values from -6 to 6
- kv_slots: int32 [16, 18], replicated, may hold values from -1 to 15, as said below
Outputs:
- out: bfloat16 [4096, 1536], P(('groups', 'ctx')), parts along dimension 0
- grad_query: bfloat16 [4096, 1536], P(('groups', 'ctx')), parts along dimension 0
- grad_key: bfloat16 [4096, 1536], P(('groups', 'ctx')), parts along dimension 0
- grad_value: bfloat16 [4096, 1536], P(('groups', 'ctx')), parts along dimension 0
There are 2 independent parts, one for each index of `groups`. A program takes and returns all parts, laid end to end along the dimension named above; an argument that names none is the same for every part. Nothing has to cross between parts.
Inputs may be any that keep to these rules, and one draw needn't show every extreme that they name: `kv_slots`: blocks are the tiles of two time planes of 4 x 2 tiles in raster order (plane, row, column). The row of block b lists, in a drawn order, b itself and a drawn subset of the blocks whose tile lies in either plane within one row and one column of b's tile; -1 fills the other entries. No block is listed twice in a row.
All inputs are finite; a program needn't handle non-finite values.
Results may differ from a plain program's by a relative error of at most 0.0065.
The roundings to bfloat16 on the way count: a program that leaves them out, or rounds other values in their place, can miss the bound.
Values may be sent and summed in bfloat16 or wider, within the bound.
No kernel may reach another device: no remote copies, remote signals or barrier semaphores. Data moves between devices by JAX's collectives and lax.ppermute only.
A program may use at most 128 MiB of HBM per device.

v0:
```python
import jax
import jax.numpy as jnp
from jax import lax
from jax.sharding import PartitionSpec as P

HEADS = 12
HEAD = 128
BLOCK = 128
TILE_H = 4


head_batch = 4
masked_score = -1e30


def from_behind(value, axis, by):
    count = lax.axis_size(axis)
    return lax.ppermute(value, axis, [(i, (i + by) % count) for i in range(count)])


def neighbour_offsets(devices, blocks, tile_width):
    plane_size = TILE_H * tile_width
    total_slots = devices * blocks
    offset_set = set()
    for plane_step in (0, 1):
        for row_step in (-1, 0, 1):
            for col_step in (-1, 0, 1):
                offset = (plane_step * plane_size + row_step * tile_width + col_step) % total_slots
                target = offset % total_slots // blocks
                if target > devices // 2:
                    target = target - devices
                if target != 0:
                    offset_set.add(target)
    return offset_set


def split_heads(tensor):
    return tensor.reshape(
        tensor.shape[0], HEADS // head_batch, head_batch, tensor.shape[1] // HEADS
    )


def pick_group(tensor, group_index):
    return lax.dynamic_index_in_dim(tensor, group_index, 1, keepdims=False)


def join_heads(stacked):
    return jnp.moveaxis(stacked, 0, 1).reshape(stacked.shape[1], -1)


def apply_mask(scores, block_mask):
    heads_here, row_total, col_total = scores.shape
    row_blocks, col_blocks = block_mask.shape
    shaped = scores.reshape(
        heads_here, row_blocks, row_total // row_blocks, col_blocks, col_total // col_blocks
    )
    shaped = jnp.where(block_mask[None, :, None, :, None], shaped, masked_score)
    return shaped.reshape(heads_here, row_total, col_total)


def forward_group(group_index, queries, keys, values, allowed, scaling):
    query_part = pick_group(queries, group_index)
    key_part = pick_group(keys, group_index)
    value_part = pick_group(values, group_index)
    scores = (
        jnp.einsum("qhd,khd->hqk", query_part, key_part, preferred_element_type=jnp.float32)
        * scaling
    )
    scores = apply_mask(scores, allowed)
    peak_score = jnp.max(scores, axis=2, keepdims=True)
    denominator = jnp.sum(jnp.exp(scores - peak_score), axis=2, keepdims=True)
    log_norm = peak_score + jnp.log(denominator)
    weights = jnp.exp(scores - log_norm).astype(jnp.bfloat16)
    mixed_rows = jnp.einsum("hqk,khd->qhd", weights, value_part, preferred_element_type=jnp.float32)
    return (mixed_rows, log_norm[:, :, 0])


def query_group(
    group_index, queries, keys, values, gradients, log_split, delta_split, allowed, scaling
):
    query_part = pick_group(queries, group_index)
    key_part = pick_group(keys, group_index)
    value_part = pick_group(values, group_index)
    grad_part = pick_group(gradients, group_index)
    log_part = jnp.transpose(pick_group(log_split, group_index))
    delta_part = jnp.transpose(pick_group(delta_split, group_index))
    scores = (
        jnp.einsum("qhd,khd->hqk", query_part, key_part, preferred_element_type=jnp.float32)
        * scaling
    )
    scores = apply_mask(scores, allowed)
    weights = jnp.exp(scores - log_part[:, :, None])
    grad_probs = jnp.einsum(
        "qhd,khd->hqk", grad_part, value_part, preferred_element_type=jnp.float32
    )
    grad_scores = (weights * (grad_probs - delta_part[:, :, None])).astype(jnp.bfloat16)
    return (
        jnp.einsum("hqk,khd->qhd", grad_scores, key_part, preferred_element_type=jnp.float32)
        * scaling
    )


def key_group(
    group_index, keys, values, queries, gradients, log_split, delta_split, back_mask, scaling
):
    key_part = pick_group(keys, group_index)
    value_part = pick_group(values, group_index)
    query_part = pick_group(queries, group_index)
    grad_part = pick_group(gradients, group_index)
    log_part = jnp.transpose(pick_group(log_split, group_index))
    delta_part = jnp.transpose(pick_group(delta_split, group_index))
    scores = (
        jnp.einsum("khd,chd->hkc", key_part, query_part, preferred_element_type=jnp.float32)
        * scaling
    )
    scores = apply_mask(scores, back_mask)
    weights = jnp.exp(scores - log_part[:, None, :])
    grad_probs = jnp.einsum(
        "khd,chd->hkc", value_part, grad_part, preferred_element_type=jnp.float32
    )
    grad_scores = (weights * (grad_probs - delta_part[:, None, :])).astype(jnp.bfloat16)
    grad_values = jnp.einsum(
        "hkc,chd->khd", weights.astype(jnp.bfloat16), grad_part, preferred_element_type=jnp.float32
    )
    grad_keys = (
        jnp.einsum("hkc,chd->khd", grad_scores, query_part, preferred_element_type=jnp.float32)
        * scaling
    )
    return (grad_keys, grad_values)


def body(query, key_rows, value, grad_out, kv_slots):
    devices = lax.axis_size("ctx")
    device_index = lax.axis_index("ctx")
    row_count = query.shape[0]
    blocks = row_count // BLOCK
    tile_width = devices * blocks // (2 * TILE_H)
    offset_set = neighbour_offsets(devices, blocks, tile_width)
    visit_order = sorted(offset_set)
    distances = [0] + visit_order
    local_slots = jnp.arange(blocks, dtype=jnp.int32)
    cand_slots = jnp.concatenate(
        [(device_index + distance) % devices * blocks + local_slots for distance in distances]
    ).astype(jnp.int32)
    own_blocks = device_index * blocks + local_slots
    own_lists = lax.dynamic_slice_in_dim(kv_slots, device_index * blocks, blocks, 0)
    allowed = jnp.any(own_lists[:, :, None] == cand_slots[None, None, :], axis=1)
    cand_lists = jnp.take(kv_slots, cand_slots, axis=0)
    back_mask = jnp.any(cand_lists[None, :, :] == own_blocks[:, None, None], axis=2)
    scaling = HEAD ** (-0.5)
    groups = HEADS // head_batch
    group_ids = jnp.arange(groups)
    arrived = [from_behind((key_rows, value), "ctx", -distance) for distance in visit_order]
    cand_keys = split_heads(jnp.concatenate([key_rows] + [item[0] for item in arrived], axis=0))
    cand_values = split_heads(jnp.concatenate([value] + [item[1] for item in arrived], axis=0))
    queries = split_heads(query)
    mixed_all, norm_all = lax.map(
        lambda group_index: forward_group(
            group_index, queries, cand_keys, cand_values, allowed, scaling
        ),
        group_ids,
    )
    out = join_heads(mixed_all).astype(jnp.bfloat16)
    log_rows = jnp.transpose(norm_all.reshape(HEADS, row_count))
    delta_rows = jnp.sum(
        (grad_out.astype(jnp.float32) * out.astype(jnp.float32)).reshape(row_count, HEADS, -1),
        axis=2,
    )
    gradients = split_heads(grad_out)
    log_split = log_rows.reshape(row_count, groups, head_batch)
    delta_split = delta_rows.reshape(row_count, groups, head_batch)
    query_terms = lax.map(
        lambda group_index: query_group(
            group_index,
            queries,
            cand_keys,
            cand_values,
            gradients,
            log_split,
            delta_split,
            allowed,
            scaling,
        ),
        group_ids,
    )
    grad_query = join_heads(query_terms).astype(jnp.bfloat16)
    returned = [from_behind((query, grad_out), "ctx", -distance) for distance in visit_order]
    cand_queries = jnp.concatenate([query] + [item[0] for item in returned], axis=0)
    cand_grads = jnp.concatenate([grad_out] + [item[1] for item in returned], axis=0)
    row_terms = [from_behind((log_rows, delta_rows), "ctx", -distance) for distance in visit_order]
    cand_log = jnp.concatenate([log_rows] + [item[0] for item in row_terms], axis=0).reshape(
        -1, groups, head_batch
    )
    cand_delta = jnp.concatenate([delta_rows] + [item[1] for item in row_terms], axis=0).reshape(
        -1, groups, head_batch
    )
    own_keys = split_heads(key_rows)
    own_values = split_heads(value)
    split_queries = split_heads(cand_queries)
    split_grads = split_heads(cand_grads)
    key_terms, value_terms = lax.map(
        lambda group_index: key_group(
            group_index,
            own_keys,
            own_values,
            split_queries,
            split_grads,
            cand_log,
            cand_delta,
            back_mask,
            scaling,
        ),
        group_ids,
    )
    grad_key = join_heads(key_terms).astype(jnp.bfloat16)
    grad_value = join_heads(value_terms).astype(jnp.bfloat16)
    return (out, grad_query, grad_key, grad_value)


def solution(mesh):
    placed = (
        P(("groups", "ctx"), None),
        P(("groups", "ctx"), None),
        P(("groups", "ctx"), None),
        P(("groups", "ctx"), None),
        P(),
    )
    return jax.shard_map(
        body,
        mesh=mesh,
        in_specs=placed,
        out_specs=(
            P(("groups", "ctx"), None),
            P(("groups", "ctx"), None),
            P(("groups", "ctx"), None),
            P(("groups", "ctx"), None),
        ),
        check_vma=False,
    )
```

profile of v0, /device:TPU:13, one launch (start us, length us, event | category | flops | bytes accessed | tf_op | source)
XLA Modules:
  0.0 700.9 jit_solution(9705418312084618958)
XLA Ops:
  21.0 60.1 %collective-permute-done.13 = bf16[128,1536]{0,1:T(8,128)(2,1)} collective-permute-done((bf16[128,1536]{0,1:T(8,128)(2,1)S(1)}, bf16[128,1536]{0,1:T(8,128)(2,1)}, u32[]{:S(2)}, u32[]{:S(2)}) %collective-permute-start.13) | collective-permute-done | bytes 393248 | tf_op jit(solution)/shard_map/ppermute | solution.py:18
  82.9 6.6 collective-permute-done.14
  90.3 7.6 %collective-permute-done.15 = bf16[128,1536]{0,1:T(8,128)(2,1)S(1)} collective-permute-done((bf16[128,1536]{0,1:T(8,128)(2,1)S(1)}, bf16[128,1536]{0,1:T(8,128)(2,1)S(1)}, u32[]{:S(2)}, u32[]{:S(2)}) %collective-permute-start.15) | collective-permute-done | bytes 393248 | tf_op jit(solution)/shard_map/ppermute | solution.py:18
  98.7 7.6 %collective-permute-done.16 = bf16[128,1536]{0,1:T(8,128)(2,1)S(1)} collective-permute-done((bf16[128,1536]{0,1:T(8,128)(2,1)S(1)}, bf16[128,1536]{0,1:T(8,128)(2,1)S(1)}, u32[]{:S(2)}, u32[]{:S(2)}) %collective-permute-start.16) | collective-permute-done | bytes 393248 | tf_op jit(solution)/shard_map/ppermute | solution.py:18
  107.1 7.6 %collective-permute-done.17 = bf16[128,1536]{0,1:T(8,128)(2,1)S(1)} collective-permute-done((bf16[128,1536]{0,1:T(8,128)(2,1)S(1)}, bf16[128,1536]{0,1:T(8,128)(2,1)S(1)}, u32[]{:S(2)}, u32[]{:S(2)}) %collective-permute-start.17) | collective-permute-done | bytes 393248 | tf_op jit(solution)/shard_map/ppermute | solution.py:18
  119.8 5.1 collective-permute-done.19
  131.0 7.6 %collective-permute-start.22 = (bf16[128,1536]{0,1:T(8,128)(2,1)S(1)}, bf16[128,1536]{0,1:T(8,128)(2,1)S(1)}, u32[]{:S(2)}, u32[]{:S(2)}) collective-permute-start(bf16[128,1536]{0,1:T(8,128)(2,1)S(1)} %copy.104), channel_id=1, source_target_pairs={{0,11},{1,12},{2,13},{3,14},{4,15},{5,0},{6,1},{7,2},{8,3},{9,4},{... | collective-permute-start | bytes 1179656 | tf_op jit(solution)/shard_map/ppermute | solution.py:18
  139.4 4.5 collective-permute-start.23
  144.8 5.7 collective-permute-done.22
  150.5 5.6 collective-permute-start.24
  159.7 30.1 %collective-permute-start.25 = (bf16[128,1536]{0,1:T(8,128)(2,1)S(1)}, bf16[128,1536]{0,1:T(8,128)(2,1)S(1)}, u32[]{:S(2)}, u32[]{:S(2)}) collective-permute-start(bf16[128,1536]{0,1:T(8,128)(2,1)S(1)} %copy.104), channel_id=1, source_target_pairs={{0,8},{1,9},{2,10},{3,11},{4,12},{5,13},{6,14},{7,15},{8,0},{9,1},... | collective-permute-start | bytes 1179656 | tf_op jit(solution)/shard_map/ppermute | solution.py:18
  191.4 7.4 %collective-permute-done.25 = bf16[128,1536]{0,1:T(8,128)(2,1)S(1)} collective-permute-done((bf16[128,1536]{0,1:T(8,128)(2,1)S(1)}, bf16[128,1536]{0,1:T(8,128)(2,1)S(1)}, u32[]{:S(2)}, u32[]{:S(2)}) %collective-permute-start.25) | collective-permute-done | bytes 393248 | tf_op jit(solution)/shard_map/ppermute | solution.py:18
  200.6 8.3 %copy.106 = bf16[1792,3,4,128]{3,0,2,1:T(8,128)(2,1)} copy(bf16[1792,3,4,128]{0,3,2,1:T(8,128)(2,1)} %bitcast.272) | data formatting | bytes 11010048 | tf_op jit(solution)/shard_map/while | solution.py:157
  208.8 9.3 %collective-permute-start.5 = (bf16[128,1536]{0,1:T(8,128)(2,1)S(1)}, bf16[128,1536]{0,1:T(8,128)(2,1)S(1)}, u32[]{:S(2)}, u32[]{:S(2)}) collective-permute-start(bf16[128,1536]{0,1:T(8,128)(2,1)S(1)} %copy.89), channel_id=1, source_target_pairs={{0,1},{1,2},{2,3},{3,4},{4,5},{5,6},{6,7},{7,8},{8,9},{9,10},{10,1... | collective-permute-start | bytes 1179656 | tf_op jit(solution)/shard_map/ppermute | solution.py:18
  224.0 4.5 collective-permute-start.8
  231.2 16.9 %collective-permute-start.10 = (bf16[128,1536]{0,1:T(8,128)(2,1)S(1)}, bf16[128,1536]{0,1:T(8,128)(2,1)S(1)}, u32[]{:S(2)}, u32[]{:S(2)}) collective-permute-start(bf16[128,1536]{0,1:T(8,128)(2,1)S(1)} %copy.89), channel_id=1, source_target_pairs={{0,10},{1,11},{2,12},{3,13},{4,14},{5,15},{6,0},{7,1},{8,2},{9,3},... | collective-permute-start | bytes 1179656 | tf_op jit(solution)/shard_map/ppermute | solution.py:18
  249.0 5.9 collective-permute-start.11
  264.7 5.6 collective-permute-start.28
  271.1 22.9 %collective-permute-start.29 = (bf16[128,1536]{0,1:T(8,128)(2,1)S(1)}, bf16[128,1536]{0,1:T(8,128)(2,1)}, u32[]{:S(2)}, u32[]{:S(2)}) collective-permute-start(bf16[128,1536]{0,1:T(8,128)(2,1)S(1)} %copy.90), channel_id=1, source_target_pairs={{0,3},{1,4},{2,5},{3,6},{4,7},{5,8},{6,9},{7,10},{8,11},{9,12},{10... | collective-permute-start | bytes 1179656 | tf_op jit(solution)/shard_map/ppermute | solution.py:18
  294.9 40.5 %collective-permute-start.30 = (bf16[128,1536]{0,1:T(8,128)(2,1)S(1)}, bf16[128,1536]{0,1:T(8,128)(2,1)}, u32[]{:S(2)}, u32[]{:S(2)}) collective-permute-start(bf16[128,1536]{0,1:T(8,128)(2,1)S(1)} %copy.90), channel_id=1, source_target_pairs={{0,2},{1,3},{2,4},{3,5},{4,6},{5,7},{6,8},{7,9},{8,10},{9,11},{10,... | collective-permute-start | bytes 1179656 | tf_op jit(solution)/shard_map/ppermute | solution.py:18
  336.2 25.4 %while.34 = (s32[]{:T(128)}, bf16[3,128,4,128]{1,3,2,0:T(8,128)(2,1)S(1)}, f32[3,4,128]{2,1,0:T(4,128)}, s32[3]{0:T(128)S(1)}, bf16[1792,3,4,128]{0,3,2,1:T(8,12...) while((s32[]{:T(128)}, ...), condition=%wide.region_4.5_spmd, body=%wide.region_1.4_spmd.sunk | while | flops 476184064 | bytes 15094717 | solution.py:157
  363.7 36.8 %while.35 = (s32[]{:T(128)}, bf16[3,128,4,128]{1,3,2,0:T(8,128)(2,1)S(1)}, s32[3]{0:T(128)S(1)}, bf16[1792,3,4,128]{3,0,2,1:T(8,128)(2,1)}, pred[1,14]{1,0:T(4,1...) while((s32[]{:T(128)}, ...), condition=%wide.region_7.8_spmd, body=%wide.region_6.7_spmd.sunk | while | flops 710213632 | bytes 13388825 | solution.py:172
  371.0 4.9 fusion.126
  383.3 5.0 fusion.126
  390.8 4.0 fusion.125
  395.5 4.9 fusion.126
  410.8 5.2 collective-permute-start.35
  425.5 9.7 %collective-permute-done.34 = bf16[128,1536]{0,1:T(8,128)(2,1)S(1)} collective-permute-done((bf16[128,1536]{0,1:T(8,128)(2,1)S(1)}, bf16[128,1536]{0,1:T(8,128)(2,1)S(1)}, u32[]{:S(2)}, u32[]{:S(2)}) %collective-permute-start.34) | collective-permute-done | bytes 393248 | tf_op jit(solution)/shard_map/ppermute | solution.py:18
  438.2 5.1 collective-permute-start.53
  448.4 30.5 %collective-permute-start.55 = (bf16[128,1536]{0,1:T(8,128)(2,1)S(1)}, bf16[128,1536]{0,1:T(8,128)(2,1)S(1)}, u32[]{:S(2)}, u32[]{:S(2)}) collective-permute-start(bf16[128,1536]{0,1:T(8,128)(2,1)S(1)} %bitcast.279), channel_id=1, source_target_pairs={{0,3},{1,4},{2,5},{3,6},{4,7},{5,8},{6,9},{7,10},{8,11},{9,12},{10... | collective-permute-start | bytes 1179656 | tf_op jit(solution)/shard_map/ppermute | solution.py:18
  479.7 38.3 %collective-permute-start.56 = (bf16[128,1536]{0,1:T(8,128)(2,1)S(1)}, bf16[128,1536]{0,1:T(8,128)(2,1)S(1)}, u32[]{:S(2)}, u32[]{:S(2)}) collective-permute-start(bf16[128,1536]{0,1:T(8,128)(2,1)S(1)} %bitcast.280), channel_id=1, source_target_pairs={{0,2},{1,3},{2,4},{3,5},{4,6},{5,7},{6,8},{7,9},{8,10},{9,11},{10,... | collective-permute-start | bytes 1179656 | tf_op jit(solution)/shard_map/ppermute | solution.py:18
  518.8 5.6 collective-permute-start.57
  530.5 20.8 %collective-permute-start.61 = (bf16[128,1536]{0,1:T(8,128)(2,1)S(1)}, bf16[128,1536]{0,1:T(8,128)(2,1)S(1)}, u32[]{:S(2)}, u32[]{:S(2)}) collective-permute-start(bf16[128,1536]{0,1:T(8,128)(2,1)S(1)} %bitcast.285), channel_id=1, source_target_pairs={{0,11},{1,12},{2,13},{3,14},{4,15},{5,0},{6,1},{7,2},{8,3},{9,4},{... | collective-permute-start | bytes 1179656 | tf_op jit(solution)/shard_map/ppermute | solution.py:18
  552.9 7.1 %collective-permute-start.63 = (bf16[128,1536]{0,1:T(8,128)(2,1)S(1)}, bf16[128,1536]{0,1:T(8,128)(2,1)S(1)}, u32[]{:S(2)}, u32[]{:S(2)}) collective-permute-start(bf16[128,1536]{0,1:T(8,128)(2,1)S(1)} %bitcast.287), channel_id=1, source_target_pairs={{0,9},{1,10},{2,11},{3,12},{4,13},{5,14},{6,15},{7,0},{8,1},{9,2},... | collective-permute-start | bytes 1179656 | tf_op jit(solution)/shard_map/ppermute | solution.py:18
  568.3 5.1 collective-permute-done.62
  577.1 24.1 %collective-permute-start.42 = (f32[128,12]{0,1:T(8,128)S(1)}, f32[128,12]{0,1:T(8,128)S(1)}, u32[]{:S(2)}, u32[]{:S(2)}) collective-permute-start(f32[128,12]{0,1:T(8,128)S(1)} %bitcast.299), channel_id=1, source_target_pairs={{0,3},{1,4},{2,5},{3,6},{4,7},{5,8},{6,9},{7,10},{8,11},{9,12},{10... | collective-permute-start | bytes 18440 | tf_op jit(solution)/shard_map/ppermute | solution.py:18
  602.0 8.8 %collective-permute-start.43 = (f32[128,12]{0,1:T(8,128)S(1)}, f32[128,12]{0,1:T(8,128)S(1)}, u32[]{:S(2)}, u32[]{:S(2)}) collective-permute-start(f32[128,12]{0,1:T(8,128)S(1)} %bitcast.300), channel_id=1, source_target_pairs={{0,2},{1,3},{2,4},{3,5},{4,6},{5,7},{6,8},{7,9},{8,10},{9,11},{10,... | collective-permute-start | bytes 18440 | tf_op jit(solution)/shard_map/ppermute | solution.py:18
  613.5 7.8 %collective-permute-start.44 = (f32[128,12]{0,1:T(8,128)S(1)}, f32[128,12]{0,1:T(8,128)S(1)}, u32[]{:S(2)}, u32[]{:S(2)}) collective-permute-start(f32[128,12]{0,1:T(8,128)S(1)} %bitcast.301), channel_id=1, source_target_pairs={{0,1},{1,2},{2,3},{3,4},{4,5},{5,6},{6,7},{7,8},{8,9},{9,10},{10,1... | collective-permute-start | bytes 18440 | tf_op jit(solution)/shard_map/ppermute | solution.py:18
  621.5 4.1 collective-permute-start.47
  625.7 4.0 collective-permute-start.49
  635.6 4.0 collective-permute-start.67
  655.1 43.9 %while.36 = (s32[]{:T(128)}, bf16[3,128,4,128]{1,3,2,0:T(8,128)(2,1)S(1)}, bf16[3,128,4,128]{1,3,2,0:T(8,128)(2,1)S(1)}, s32[3]{0:T(128)S(1)}, bf16[1792,3,4,128...) while((s32[]{:T(128)}, ...), condition=%wide.region_10.11_spmd, body=%wide.region_9.10_spmd.sunk | while | flops 946012160 | bytes 19315668 | solution.py:201
  657.8 4.4 subtract_exponential_fusion.2
  662.1 4.4 fusion.134
  672.4 4.4 subtract_exponential_fusion.2
  676.8 4.4 fusion.134
  687.0 4.4 subtract_exponential_fusion.2
  691.4 4.4 fusion.134
  (294 shorter events, 187.7 us)
Async XLA Ops:
  1.9 207.0 %collective-permute-start = (bf16[128,1536]{0,1:T(8,128)(2,1)S(1)}, bf16[128,1536]{0,1:T(8,128)(2,1)S(1)}, u32[]{:S(2)}, u32[]{:S(2)}) collective-permute-start(bf16[128,1536]{0,1:T(8,128)(2,1)S(1)} %copy.89), channel_id=1, source_target_pairs={{0,7},{1,8},{2,9},{3,10},{4,11},{5,12},{6,13},{7,14},{8,15},{9,0},... | collective-permute-start | bytes 1179656 | tf_op jit(solution)/shard_map/ppermute | solution.py:18
  4.8 214.1 %collective-permute-start.1 = (bf16[128,1536]{0,1:T(8,128)(2,1)S(1)}, bf16[128,1536]{0,1:T(8,128)(2,1)S(1)}, u32[]{:S(2)}, u32[]{:S(2)}) collective-permute-start(bf16[128,1536]{0,1:T(8,128)(2,1)S(1)} %copy.89), channel_id=1, source_target_pairs={{0,6},{1,7},{2,8},{3,9},{4,10},{5,11},{6,12},{7,13},{8,14},{9,15},... | collective-permute-start | bytes 1179656 | tf_op jit(solution)/shard_map/ppermute | solution.py:18
  4.8 215.0 %collective-permute-start.2 = (bf16[128,1536]{0,1:T(8,128)(2,1)S(1)}, bf16[128,1536]{0,1:T(8,128)(2,1)S(1)}, u32[]{:S(2)}, u32[]{:S(2)}) collective-permute-start(bf16[128,1536]{0,1:T(8,128)(2,1)S(1)} %copy.89), channel_id=1, source_target_pairs={{0,5},{1,6},{2,7},{3,8},{4,9},{5,10},{6,11},{7,12},{8,13},{9,14},{... | collective-permute-start | bytes 1179656 | tf_op jit(solution)/shard_map/ppermute | solution.py:18
  9.1 71.9 %collective-permute-start.13 = (bf16[128,1536]{0,1:T(8,128)(2,1)S(1)}, bf16[128,1536]{0,1:T(8,128)(2,1)}, u32[]{:S(2)}, u32[]{:S(2)}) collective-permute-start(bf16[128,1536]{0,1:T(8,128)(2,1)S(1)} %copy.104), channel_id=1, source_target_pairs={{0,7},{1,8},{2,9},{3,10},{4,11},{5,12},{6,13},{7,14},{8,15},{9,0},... | collective-permute-start | bytes 1179656 | tf_op jit(solution)/shard_map/ppermute | solution.py:18
  9.2 80.3 %collective-permute-start.14 = (bf16[128,1536]{0,1:T(8,128)(2,1)S(1)}, bf16[128,1536]{0,1:T(8,128)(2,1)S(1)}, u32[]{:S(2)}, u32[]{:S(2)}) collective-permute-start(bf16[128,1536]{0,1:T(8,128)(2,1)S(1)} %copy.104), channel_id=1, source_target_pairs={{0,6},{1,7},{2,8},{3,9},{4,10},{5,11},{6,12},{7,13},{8,14},{9,15},... | collective-permute-start | bytes 1179656 | tf_op jit(solution)/shard_map/ppermute | solution.py:18
  131.0 19.5 %collective-permute-start.22 = (bf16[128,1536]{0,1:T(8,128)(2,1)S(1)}, bf16[128,1536]{0,1:T(8,128)(2,1)S(1)}, u32[]{:S(2)}, u32[]{:S(2)}) collective-permute-start(bf16[128,1536]{0,1:T(8,128)(2,1)S(1)} %copy.104), channel_id=1, source_target_pairs={{0,11},{1,12},{2,13},{3,14},{4,15},{5,0},{6,1},{7,2},{8,3},{9,4},{... | collective-permute-start | bytes 1179656 | tf_op jit(solution)/shard_map/ppermute | solution.py:18
  139.4 20.2 %collective-permute-start.23 = (bf16[128,1536]{0,1:T(8,128)(2,1)S(1)}, bf16[128,1536]{0,1:T(8,128)(2,1)S(1)}, u32[]{:S(2)}, u32[]{:S(2)}) collective-permute-start(bf16[128,1536]{0,1:T(8,128)(2,1)S(1)} %copy.104), channel_id=1, source_target_pairs={{0,10},{1,11},{2,12},{3,13},{4,14},{5,15},{6,0},{7,1},{8,2},{9,3},... | collective-permute-start | bytes 1179656 | tf_op jit(solution)/shard_map/ppermute | solution.py:18
  150.5 40.1 %collective-permute-start.24 = (bf16[128,1536]{0,1:T(8,128)(2,1)S(1)}, bf16[128,1536]{0,1:T(8,128)(2,1)S(1)}, u32[]{:S(2)}, u32[]{:S(2)}) collective-permute-start(bf16[128,1536]{0,1:T(8,128)(2,1)S(1)} %copy.104), channel_id=1, source_target_pairs={{0,9},{1,10},{2,11},{3,12},{4,13},{5,14},{6,15},{7,0},{8,1},{9,2},... | collective-permute-start | bytes 1179656 | tf_op jit(solution)/shard_map/ppermute | solution.py:18
  159.7 39.2 %collective-permute-start.25 = (bf16[128,1536]{0,1:T(8,128)(2,1)S(1)}, bf16[128,1536]{0,1:T(8,128)(2,1)S(1)}, u32[]{:S(2)}, u32[]{:S(2)}) collective-permute-start(bf16[128,1536]{0,1:T(8,128)(2,1)S(1)} %copy.104), channel_id=1, source_target_pairs={{0,8},{1,9},{2,10},{3,11},{4,12},{5,13},{6,14},{7,15},{8,0},{9,1},... | collective-permute-start | bytes 1179656 | tf_op jit(solution)/shard_map/ppermute | solution.py:18
  190.6 33.4 %collective-permute-start.3 = (bf16[128,1536]{0,1:T(8,128)(2,1)S(1)}, bf16[128,1536]{0,1:T(8,128)(2,1)S(1)}, u32[]{:S(2)}, u32[]{:S(2)}) collective-permute-start(bf16[128,1536]{0,1:T(8,128)(2,1)S(1)} %copy.89), channel_id=1, source_target_pairs={{0,3},{1,4},{2,5},{3,6},{4,7},{5,8},{6,9},{7,10},{8,11},{9,12},{10... | collective-permute-start | bytes 1179656 | tf_op jit(solution)/shard_map/ppermute | solution.py:18
  198.8 30.5 %collective-permute-start.4 = (bf16[128,1536]{0,1:T(8,128)(2,1)S(1)}, bf16[128,1536]{0,1:T(8,128)(2,1)}, u32[]{:S(2)}, u32[]{:S(2)}) collective-permute-start(bf16[128,1536]{0,1:T(8,128)(2,1)S(1)} %copy.89), channel_id=1, source_target_pairs={{0,2},{1,3},{2,4},{3,5},{4,6},{5,7},{6,8},{7,9},{8,10},{9,11},{10,... | collective-permute-start | bytes 1179656 | tf_op jit(solution)/shard_map/ppermute | solution.py:18
  208.8 22.4 %collective-permute-start.5 = (bf16[128,1536]{0,1:T(8,128)(2,1)S(1)}, bf16[128,1536]{0,1:T(8,128)(2,1)S(1)}, u32[]{:S(2)}, u32[]{:S(2)}) collective-permute-start(bf16[128,1536]{0,1:T(8,128)(2,1)S(1)} %copy.89), channel_id=1, source_target_pairs={{0,1},{1,2},{2,3},{3,4},{4,5},{5,6},{6,7},{7,8},{8,9},{9,10},{10,1... | collective-permute-start | bytes 1179656 | tf_op jit(solution)/shard_map/ppermute | solution.py:18
  218.9 30.0 %collective-permute-start.6 = (bf16[128,1536]{0,1:T(8,128)(2,1)S(1)}, bf16[128,1536]{0,1:T(8,128)(2,1)S(1)}, u32[]{:S(2)}, u32[]{:S(2)}) collective-permute-start(bf16[128,1536]{0,1:T(8,128)(2,1)S(1)} %copy.89), channel_id=1, source_target_pairs={{0,15},{1,0},{2,1},{3,2},{4,3},{5,4},{6,5},{7,6},{8,7},{9,8},{10,9... | collective-permute-start | bytes 1179656 | tf_op jit(solution)/shard_map/ppermute | solution.py:18
  219.8 36.0 %collective-permute-start.7 = (bf16[128,1536]{0,1:T(8,128)(2,1)S(1)}, bf16[128,1536]{0,1:T(8,128)(2,1)S(1)}, u32[]{:S(2)}, u32[]{:S(2)}) collective-permute-start(bf16[128,1536]{0,1:T(8,128)(2,1)S(1)} %copy.89), channel_id=1, source_target_pairs={{0,14},{1,15},{2,0},{3,1},{4,2},{5,3},{6,4},{7,5},{8,6},{9,7},{10,... | collective-permute-start | bytes 1179656 | tf_op jit(solution)/shard_map/ppermute | solution.py:18
  224.0 32.6 %collective-permute-start.8 = (bf16[128,1536]{0,1:T(8,128)(2,1)S(1)}, bf16[128,1536]{0,1:T(8,128)(2,1)S(1)}, u32[]{:S(2)}, u32[]{:S(2)}) collective-permute-start(bf16[128,1536]{0,1:T(8,128)(2,1)S(1)} %copy.89), channel_id=1, source_target_pairs={{0,13},{1,14},{2,15},{3,0},{4,1},{5,2},{6,3},{7,4},{8,5},{9,6},{10... | collective-permute-start | bytes 1179656 | tf_op jit(solution)/shard_map/ppermute | solution.py:18
  229.4 32.7 %collective-permute-start.9 = (bf16[128,1536]{0,1:T(8,128)(2,1)S(1)}, bf16[128,1536]{0,1:T(8,128)(2,1)S(1)}, u32[]{:S(2)}, u32[]{:S(2)}) collective-permute-start(bf16[128,1536]{0,1:T(8,128)(2,1)S(1)} %copy.89), channel_id=1, source_target_pairs={{0,11},{1,12},{2,13},{3,14},{4,15},{5,0},{6,1},{7,2},{8,3},{9,4},{... | collective-permute-start | bytes 1179656 | tf_op jit(solution)/shard_map/ppermute | solution.py:18
  231.2 33.5 %collective-permute-start.10 = (bf16[128,1536]{0,1:T(8,128)(2,1)S(1)}, bf16[128,1536]{0,1:T(8,128)(2,1)S(1)}, u32[]{:S(2)}, u32[]{:S(2)}) collective-permute-start(bf16[128,1536]{0,1:T(8,128)(2,1)S(1)} %copy.89), channel_id=1, source_target_pairs={{0,10},{1,11},{2,12},{3,13},{4,14},{5,15},{6,0},{7,1},{8,2},{9,3},... | collective-permute-start | bytes 1179656 | tf_op jit(solution)/shard_map/ppermute | solution.py:18
  249.0 22.2 %collective-permute-start.11 = (bf16[128,1536]{0,1:T(8,128)(2,1)S(1)}, bf16[128,1536]{0,1:T(8,128)(2,1)S(1)}, u32[]{:S(2)}, u32[]{:S(2)}) collective-permute-start(bf16[128,1536]{0,1:T(8,128)(2,1)S(1)} %copy.89), channel_id=1, source_target_pairs={{0,9},{1,10},{2,11},{3,12},{4,13},{5,14},{6,15},{7,0},{8,1},{9,2},... | collective-permute-start | bytes 1179656 | tf_op jit(solution)/shard_map/ppermute | solution.py:18
  255.7 39.2 %collective-permute-start.12 = (bf16[128,1536]{0,1:T(8,128)(2,1)S(1)}, bf16[128,1536]{0,1:T(8,128)(2,1)S(1)}, u32[]{:S(2)}, u32[]{:S(2)}) collective-permute-start(bf16[128,1536]{0,1:T(8,128)(2,1)S(1)} %copy.89), channel_id=1, source_target_pairs={{0,8},{1,9},{2,10},{3,11},{4,12},{5,13},{6,14},{7,15},{8,0},{9,1},... | collective-permute-start | bytes 1179656 | tf_op jit(solution)/shard_map/ppermute | solution.py:18
  256.6 143.9 %collective-permute-start.26 = (bf16[128,1536]{0,1:T(8,128)(2,1)S(1)}, bf16[128,1536]{0,1:T(8,128)(2,1)S(1)}, u32[]{:S(2)}, u32[]{:S(2)}) collective-permute-start(bf16[128,1536]{0,1:T(8,128)(2,1)S(1)} %copy.90), channel_id=1, source_target_pairs={{0,7},{1,8},{2,9},{3,10},{4,11},{5,12},{6,13},{7,14},{8,15},{9,0},... | collective-permute-start | bytes 1179656 | tf_op jit(solution)/shard_map/ppermute | solution.py:18
  262.1 141.3 %collective-permute-start.27 = (bf16[128,1536]{0,1:T(8,128)(2,1)S(1)}, bf16[128,1536]{0,1:T(8,128)(2,1)}, u32[]{:S(2)}, u32[]{:S(2)}) collective-permute-start(bf16[128,1536]{0,1:T(8,128)(2,1)S(1)} %copy.90), channel_id=1, source_target_pairs={{0,6},{1,7},{2,8},{3,9},{4,10},{5,11},{6,12},{7,13},{8,14},{9,15},... | collective-permute-start | bytes 1179656 | tf_op jit(solution)/shard_map/ppermute | solution.py:18
  264.7 140.8 %collective-permute-start.28 = (bf16[128,1536]{0,1:T(8,128)(2,1)S(1)}, bf16[128,1536]{0,1:T(8,128)(2,1)}, u32[]{:S(2)}, u32[]{:S(2)}) collective-permute-start(bf16[128,1536]{0,1:T(8,128)(2,1)S(1)} %copy.90), channel_id=1, source_target_pairs={{0,5},{1,6},{2,7},{3,8},{4,9},{5,10},{6,11},{7,12},{8,13},{9,14},{... | collective-permute-start | bytes 1179656 | tf_op jit(solution)/shard_map/ppermute | solution.py:18
  271.1 137.6 %collective-permute-start.29 = (bf16[128,1536]{0,1:T(8,128)(2,1)S(1)}, bf16[128,1536]{0,1:T(8,128)(2,1)}, u32[]{:S(2)}, u32[]{:S(2)}) collective-permute-start(bf16[128,1536]{0,1:T(8,128)(2,1)S(1)} %copy.90), channel_id=1, source_target_pairs={{0,3},{1,4},{2,5},{3,6},{4,7},{5,8},{6,9},{7,10},{8,11},{9,12},{10... | collective-permute-start | bytes 1179656 | tf_op jit(solution)/shard_map/ppermute | solution.py:18
  294.9 115.9 %collective-permute-start.30 = (bf16[128,1536]{0,1:T(8,128)(2,1)S(1)}, bf16[128,1536]{0,1:T(8,128)(2,1)}, u32[]{:S(2)}, u32[]{:S(2)}) collective-permute-start(bf16[128,1536]{0,1:T(8,128)(2,1)S(1)} %copy.90), channel_id=1, source_target_pairs={{0,2},{1,3},{2,4},{3,5},{4,6},{5,7},{6,8},{7,9},{8,10},{9,11},{10,... | collective-permute-start | bytes 1179656 | tf_op jit(solution)/shard_map/ppermute | solution.py:18
  405.6 18.7 %collective-permute-start.33 = (bf16[128,1536]{0,1:T(8,128)(2,1)S(1)}, bf16[128,1536]{0,1:T(8,128)(2,1)S(1)}, u32[]{:S(2)}, u32[]{:S(2)}) collective-permute-start(bf16[128,1536]{0,1:T(8,128)(2,1)S(1)} %copy.90), channel_id=1, source_target_pairs={{0,14},{1,15},{2,0},{3,1},{4,2},{5,3},{6,4},{7,5},{8,6},{9,7},{10,... | collective-permute-start | bytes 1179656 | tf_op jit(solution)/shard_map/ppermute | solution.py:18
  408.7 26.4 %collective-permute-start.34 = (bf16[128,1536]{0,1:T(8,128)(2,1)S(1)}, bf16[128,1536]{0,1:T(8,128)(2,1)S(1)}, u32[]{:S(2)}, u32[]{:S(2)}) collective-permute-start(bf16[128,1536]{0,1:T(8,128)(2,1)S(1)} %copy.90), channel_id=1, source_target_pairs={{0,13},{1,14},{2,15},{3,0},{4,1},{5,2},{6,3},{7,4},{8,5},{9,6},{10... | collective-permute-start | bytes 1179656 | tf_op jit(solution)/shard_map/ppermute | solution.py:18
  410.8 27.4 %collective-permute-start.35 = (bf16[128,1536]{0,1:T(8,128)(2,1)S(1)}, bf16[128,1536]{0,1:T(8,128)(2,1)S(1)}, u32[]{:S(2)}, u32[]{:S(2)}) collective-permute-start(bf16[128,1536]{0,1:T(8,128)(2,1)S(1)} %copy.90), channel_id=1, source_target_pairs={{0,11},{1,12},{2,13},{3,14},{4,15},{5,0},{6,1},{7,2},{8,3},{9,4},{... | collective-permute-start | bytes 1179656 | tf_op jit(solution)/shard_map/ppermute | solution.py:18
  417.9 26.2 %collective-permute-start.36 = (bf16[128,1536]{0,1:T(8,128)(2,1)S(1)}, bf16[128,1536]{0,1:T(8,128)(2,1)S(1)}, u32[]{:S(2)}, u32[]{:S(2)}) collective-permute-start(bf16[128,1536]{0,1:T(8,128)(2,1)S(1)} %copy.90), channel_id=1, source_target_pairs={{0,10},{1,11},{2,12},{3,13},{4,14},{5,15},{6,0},{7,1},{8,2},{9,3},... | collective-permute-start | bytes 1179656 | tf_op jit(solution)/shard_map/ppermute | solution.py:18
  419.7 28.7 %collective-permute-start.37 = (bf16[128,1536]{0,1:T(8,128)(2,1)S(1)}, bf16[128,1536]{0,1:T(8,128)(2,1)S(1)}, u32[]{:S(2)}, u32[]{:S(2)}) collective-permute-start(bf16[128,1536]{0,1:T(8,128)(2,1)S(1)} %copy.90), channel_id=1, source_target_pairs={{0,9},{1,10},{2,11},{3,12},{4,13},{5,14},{6,15},{7,0},{8,1},{9,2},... | collective-permute-start | bytes 1179656 | tf_op jit(solution)/shard_map/ppermute | solution.py:18
  424.3 55.4 %collective-permute-start.38 = (bf16[128,1536]{0,1:T(8,128)(2,1)S(1)}, bf16[128,1536]{0,1:T(8,128)(2,1)S(1)}, u32[]{:S(2)}, u32[]{:S(2)}) collective-permute-start(bf16[128,1536]{0,1:T(8,128)(2,1)S(1)} %copy.90), channel_id=1, source_target_pairs={{0,8},{1,9},{2,10},{3,11},{4,12},{5,13},{6,14},{7,15},{8,0},{9,1},... | collective-permute-start | bytes 1179656 | tf_op jit(solution)/shard_map/ppermute | solution.py:18
  435.2 83.7 %collective-permute-start.52 = (bf16[128,1536]{0,1:T(8,128)(2,1)S(1)}, bf16[128,1536]{0,1:T(8,128)(2,1)S(1)}, u32[]{:S(2)}, u32[]{:S(2)}) collective-permute-start(bf16[128,1536]{0,1:T(8,128)(2,1)S(1)} %bitcast.276), channel_id=1, source_target_pairs={{0,7},{1,8},{2,9},{3,10},{4,11},{5,12},{6,13},{7,14},{8,15},{9,0},... | collective-permute-start | bytes 1179656 | tf_op jit(solution)/shard_map/ppermute | solution.py:18
  438.2 87.0 %collective-permute-start.53 = (bf16[128,1536]{0,1:T(8,128)(2,1)S(1)}, bf16[128,1536]{0,1:T(8,128)(2,1)S(1)}, u32[]{:S(2)}, u32[]{:S(2)}) collective-permute-start(bf16[128,1536]{0,1:T(8,128)(2,1)S(1)} %bitcast.277), channel_id=1, source_target_pairs={{0,6},{1,7},{2,8},{3,9},{4,10},{5,11},{6,12},{7,13},{8,14},{9,15},... | collective-permute-start | bytes 1179656 | tf_op jit(solution)/shard_map/ppermute | solution.py:18
  444.0 82.4 %collective-permute-start.54 = (bf16[128,1536]{0,1:T(8,128)(2,1)S(1)}, bf16[128,1536]{0,1:T(8,128)(2,1)S(1)}, u32[]{:S(2)}, u32[]{:S(2)}) collective-permute-start(bf16[128,1536]{0,1:T(8,128)(2,1)S(1)} %bitcast.278), channel_id=1, source_target_pairs={{0,5},{1,6},{2,7},{3,8},{4,9},{5,10},{6,11},{7,12},{8,13},{9,14},{... | collective-permute-start | bytes 1179656 | tf_op jit(solution)/shard_map/ppermute | solution.py:18
  448.4 80.3 %collective-permute-start.55 = (bf16[128,1536]{0,1:T(8,128)(2,1)S(1)}, bf16[128,1536]{0,1:T(8,128)(2,1)S(1)}, u32[]{:S(2)}, u32[]{:S(2)}) collective-permute-start(bf16[128,1536]{0,1:T(8,128)(2,1)S(1)} %bitcast.279), channel_id=1, source_target_pairs={{0,3},{1,4},{2,5},{3,6},{4,7},{5,8},{6,9},{7,10},{8,11},{9,12},{10... | collective-permute-start | bytes 1179656 | tf_op jit(solution)/shard_map/ppermute | solution.py:18
  479.7 50.8 %collective-permute-start.56 = (bf16[128,1536]{0,1:T(8,128)(2,1)S(1)}, bf16[128,1536]{0,1:T(8,128)(2,1)S(1)}, u32[]{:S(2)}, u32[]{:S(2)}) collective-permute-start(bf16[128,1536]{0,1:T(8,128)(2,1)S(1)} %bitcast.280), channel_id=1, source_target_pairs={{0,2},{1,3},{2,4},{3,5},{4,6},{5,7},{6,8},{7,9},{8,10},{9,11},{10,... | collective-permute-start | bytes 1179656 | tf_op jit(solution)/shard_map/ppermute | solution.py:18
  518.8 33.2 %collective-permute-start.57 = (bf16[128,1536]{0,1:T(8,128)(2,1)S(1)}, bf16[128,1536]{0,1:T(8,128)(2,1)S(1)}, u32[]{:S(2)}, u32[]{:S(2)}) collective-permute-start(bf16[128,1536]{0,1:T(8,128)(2,1)S(1)} %bitcast.281), channel_id=1, source_target_pairs={{0,1},{1,2},{2,3},{3,4},{4,5},{5,6},{6,7},{7,8},{8,9},{9,10},{10,1... | collective-permute-start | bytes 1179656 | tf_op jit(solution)/shard_map/ppermute | solution.py:18
  525.2 27.7 %collective-permute-start.58 = (bf16[128,1536]{0,1:T(8,128)(2,1)S(1)}, bf16[128,1536]{0,1:T(8,128)(2,1)S(1)}, u32[]{:S(2)}, u32[]{:S(2)}) collective-permute-start(bf16[128,1536]{0,1:T(8,128)(2,1)S(1)} %bitcast.282), channel_id=1, source_target_pairs={{0,15},{1,0},{2,1},{3,2},{4,3},{5,4},{6,5},{7,6},{8,7},{9,8},{10,9... | collective-permute-start | bytes 1179656 | tf_op jit(solution)/shard_map/ppermute | solution.py:18
  526.5 34.4 %collective-permute-start.59 = (bf16[128,1536]{0,1:T(8,128)(2,1)S(1)}, bf16[128,1536]{0,1:T(8,128)(2,1)S(1)}, u32[]{:S(2)}, u32[]{:S(2)}) collective-permute-start(bf16[128,1536]{0,1:T(8,128)(2,1)S(1)} %bitcast.283), channel_id=1, source_target_pairs={{0,14},{1,15},{2,0},{3,1},{4,2},{5,3},{6,4},{7,5},{8,6},{9,7},{10,... | collective-permute-start | bytes 1179656 | tf_op jit(solution)/shard_map/ppermute | solution.py:18
  528.7 33.0 %collective-permute-start.60 = (bf16[128,1536]{0,1:T(8,128)(2,1)S(1)}, bf16[128,1536]{0,1:T(8,128)(2,1)S(1)}, u32[]{:S(2)}, u32[]{:S(2)}) collective-permute-start(bf16[128,1536]{0,1:T(8,128)(2,1)S(1)} %bitcast.284), channel_id=1, source_target_pairs={{0,13},{1,14},{2,15},{3,0},{4,1},{5,2},{6,3},{7,4},{8,5},{9,6},{10... | collective-permute-start | bytes 1179656 | tf_op jit(solution)/shard_map/ppermute | solution.py:18
  530.5 33.8 %collective-permute-start.61 = (bf16[128,1536]{0,1:T(8,128)(2,1)S(1)}, bf16[128,1536]{0,1:T(8,128)(2,1)S(1)}, u32[]{:S(2)}, u32[]{:S(2)}) collective-permute-start(bf16[128,1536]{0,1:T(8,128)(2,1)S(1)} %bitcast.285), channel_id=1, source_target_pairs={{0,11},{1,12},{2,13},{3,14},{4,15},{5,0},{6,1},{7,2},{8,3},{9,4},{... | collective-permute-start | bytes 1179656 | tf_op jit(solution)/shard_map/ppermute | solution.py:18
  552.0 21.3 %collective-permute-start.62 = (bf16[128,1536]{0,1:T(8,128)(2,1)S(1)}, bf16[128,1536]{0,1:T(8,128)(2,1)S(1)}, u32[]{:S(2)}, u32[]{:S(2)}) collective-permute-start(bf16[128,1536]{0,1:T(8,128)(2,1)S(1)} %bitcast.286), channel_id=1, source_target_pairs={{0,10},{1,11},{2,12},{3,13},{4,14},{5,15},{6,0},{7,1},{8,2},{9,3},... | collective-permute-start | bytes 1179656 | tf_op jit(solution)/shard_map/ppermute | solution.py:18
  552.9 24.2 %collective-permute-start.63 = (bf16[128,1536]{0,1:T(8,128)(2,1)S(1)}, bf16[128,1536]{0,1:T(8,128)(2,1)S(1)}, u32[]{:S(2)}, u32[]{:S(2)}) collective-permute-start(bf16[128,1536]{0,1:T(8,128)(2,1)S(1)} %bitcast.287), channel_id=1, source_target_pairs={{0,9},{1,10},{2,11},{3,12},{4,13},{5,14},{6,15},{7,0},{8,1},{9,2},... | collective-permute-start | bytes 1179656 | tf_op jit(solution)/shard_map/ppermute | solution.py:18
  560.8 41.2 %collective-permute-start.64 = (bf16[128,1536]{0,1:T(8,128)(2,1)S(1)}, bf16[128,1536]{0,1:T(8,128)(2,1)S(1)}, u32[]{:S(2)}, u32[]{:S(2)}) collective-permute-start(bf16[128,1536]{0,1:T(8,128)(2,1)S(1)} %bitcast.288), channel_id=1, source_target_pairs={{0,8},{1,9},{2,10},{3,11},{4,12},{5,13},{6,14},{7,15},{8,0},{9,1},... | collective-permute-start | bytes 1179656 | tf_op jit(solution)/shard_map/ppermute | solution.py:18
  561.6 51.9 %collective-permute-start.39 = (f32[128,12]{0,1:T(8,128)S(1)}, f32[128,12]{0,1:T(8,128)S(1)}, u32[]{:S(2)}, u32[]{:S(2)}) collective-permute-start(f32[128,12]{0,1:T(8,128)S(1)} %bitcast.296), channel_id=1, source_target_pairs={{0,7},{1,8},{2,9},{3,10},{4,11},{5,12},{6,13},{7,14},{8,15},{9,0},... | collective-permute-start | bytes 18440 | tf_op jit(solution)/shard_map/ppermute | solution.py:18
  564.2 57.2 %collective-permute-start.40 = (f32[128,12]{0,1:T(8,128)S(1)}, f32[128,12]{0,1:T(8,128)S(1)}, u32[]{:S(2)}, u32[]{:S(2)}) collective-permute-start(f32[128,12]{0,1:T(8,128)S(1)} %bitcast.297), channel_id=1, source_target_pairs={{0,6},{1,7},{2,8},{3,9},{4,10},{5,11},{6,12},{7,13},{8,14},{9,15},... | collective-permute-start | bytes 18440 | tf_op jit(solution)/shard_map/ppermute | solution.py:18
  573.4 48.0 %collective-permute-start.41 = (f32[128,12]{0,1:T(8,128)S(1)}, f32[128,12]{0,1:T(8,128)S(1)}, u32[]{:S(2)}, u32[]{:S(2)}) collective-permute-start(f32[128,12]{0,1:T(8,128)S(1)} %bitcast.298), channel_id=1, source_target_pairs={{0,5},{1,6},{2,7},{3,8},{4,9},{5,10},{6,11},{7,12},{8,13},{9,14},{... | collective-permute-start | bytes 18440 | tf_op jit(solution)/shard_map/ppermute | solution.py:18
  577.1 44.4 %collective-permute-start.42 = (f32[128,12]{0,1:T(8,128)S(1)}, f32[128,12]{0,1:T(8,128)S(1)}, u32[]{:S(2)}, u32[]{:S(2)}) collective-permute-start(f32[128,12]{0,1:T(8,128)S(1)} %bitcast.299), channel_id=1, source_target_pairs={{0,3},{1,4},{2,5},{3,6},{4,7},{5,8},{6,9},{7,10},{8,11},{9,12},{10... | collective-permute-start | bytes 18440 | tf_op jit(solution)/shard_map/ppermute | solution.py:18
  602.0 23.6 %collective-permute-start.43 = (f32[128,12]{0,1:T(8,128)S(1)}, f32[128,12]{0,1:T(8,128)S(1)}, u32[]{:S(2)}, u32[]{:S(2)}) collective-permute-start(f32[128,12]{0,1:T(8,128)S(1)} %bitcast.300), channel_id=1, source_target_pairs={{0,2},{1,3},{2,4},{3,5},{4,6},{5,7},{6,8},{7,9},{8,10},{9,11},{10,... | collective-permute-start | bytes 18440 | tf_op jit(solution)/shard_map/ppermute | solution.py:18
  (37 other events, 461.7 us)
where the time goes:
time: 705 us; the launch traced here: 701 us
  starting transfers between devices  382 us (54%)
  waiting for transfers between devices  137 us (19%)
  local copies, waits for them, and re-layouts  81 us (11%)
  matrix products  76.5 us (11%)
  loops' own time  17.8 us (3%)
    ppermute x78, starting transfers between devices, from_behind(): lax.ppermute(value, axis, [(i, (i + by) % count) for i in range(count)])  382 us
    ppermute x78, waiting for transfers between devices, from_behind(): lax.ppermute(value, axis, [(i, (i + by) % count) for i in range(count)])  137 us
    unnamed x91, local copies, waits for them, and re-layouts  55.4 us
    dot_general x3, matrix products, query_group(): jnp.einsum('hqk,khd->qhd', grad_scores, key_part, preferred_element_type=...  14.8 us
  transfers between devices with their start and end apart: 78, of which 17 were waited for; matrix products, arithmetic and copies ran while one was open for 17% of the time, Pallas kernels for 0%

commit v1 on v0

--- a/solution.py
+++ b/solution.py
@@ -1,16 +1,226 @@
+import functools
+
 import jax
 import jax.numpy as jnp
 from jax import lax
+from jax.experimental import pallas as pl
+from jax.experimental.pallas import tpu as pltpu
 from jax.sharding import PartitionSpec as P
 
 HEADS = 12
 HEAD = 128
 BLOCK = 128
 TILE_H = 4
-
+PLANES = 2
 
 head_batch = 4
 masked_score = -1e30
+log2_e = 1.4426950408889634
+
+
+def nt_dot(left, right):
+    return lax.dot_general(
+        left, right, (((1,), (1,)), ((), ())), preferred_element_type=jnp.float32
+    )
+
+
+def nn_dot(left, right):
+    return lax.dot_general(
+        left, right, (((1,), (0,)), ((), ())), preferred_element_type=jnp.float32
+    )
+
+
+def key_rows_of(row):
+    return jnp.maximum(row - 1, 0), jnp.minimum(row + 2, TILE_H)
+
+
+def row_blocks(width, row):
+    return [plane * TILE_H * width + row * width + col for plane in range(PLANES) for col in range(width)]
+
+
+def query_places(width):
+    return PLANES * TILE_H, width * BLOCK
+
+
+def forward_kernel(width, kvq_ref, bias_ref, out_ref, log_ref, score_ref, vt_ref):
+    blocks = PLANES * TILE_H * width
+    steps, lanes = query_places(width)
+    scale = HEAD ** (-0.5) * log2_e
+    for block in range(blocks):
+        vt_ref[block] = jnp.transpose(kvq_ref[block, 1])
+
+    def step(place, _):
+        row = place % TILE_H
+        first = place * width
+        queries = kvq_ref[pl.ds(first, width), 2].reshape(lanes, HEAD)
+        low, high = key_rows_of(row)
+
+        def scores_of(key_row, peak):
+            for block in row_blocks(width, key_row):
+                scores = nt_dot(kvq_ref[block, 0], queries) * scale
+                scores = scores + bias_ref[block, place]
+                score_ref[block] = scores
+                peak = jnp.maximum(peak, jnp.max(scores.reshape(-1, 8, lanes), axis=0))
+            return peak
+
+        peak = lax.fori_loop(low, high, scores_of, jnp.full((8, lanes), masked_score, jnp.float32))
+        peak = jnp.max(peak, axis=0, keepdims=True)
+
+        def total_of(key_row, total):
+            for block in row_blocks(width, key_row):
+                power = jnp.exp2(score_ref[block] - peak)
+                score_ref[block] = power
+                total = total + jnp.sum(power.reshape(-1, 8, lanes), axis=0)
+            return total
+
+        total = lax.fori_loop(low, high, total_of, jnp.zeros((8, lanes), jnp.float32))
+        total = jnp.sum(total, axis=0, keepdims=True)
+        inverse = 1.0 / total
+        log_ref[place] = jnp.broadcast_to(peak + jnp.log2(total), (8, lanes))
+
+        def mixed_of(key_row, mixed):
+            for block in row_blocks(width, key_row):
+                weights = (score_ref[block] * inverse).astype(jnp.bfloat16)
+                mixed = mixed + nn_dot(vt_ref[block], weights)
+            return mixed
+
+        mixed = lax.fori_loop(low, high, mixed_of, jnp.zeros((HEAD, lanes), jnp.float32))
+        out_ref[pl.ds(first, width)] = (
+            jnp.transpose(mixed).astype(jnp.bfloat16).reshape(width, BLOCK, HEAD)
+        )
+        return 0
+
+    lax.fori_loop(0, steps, step, 0)
+
+
+def backward_kernel(
+    width, kvq_ref, grad_ref, out_ref, log_ref, bias_ref, terms_ref, kt_ref, key_acc, value_acc
+):
+    blocks = PLANES * TILE_H * width
+    steps, lanes = query_places(width)
+    factor = HEAD ** (-0.5)
+    scale = factor * log2_e
+    for block in range(blocks):
+        kt_ref[block] = jnp.transpose(kvq_ref[block, 0])
+    key_acc[...] = jnp.zeros_like(key_acc)
+    value_acc[...] = jnp.zeros_like(value_acc)
+
+    def step(place, _):
+        row = place % TILE_H
+        first = place * width
+        queries = kvq_ref[pl.ds(first, width), 2].reshape(lanes, HEAD)
+        grads = grad_ref[pl.ds(first, width)].reshape(lanes, HEAD)
+        outs = out_ref[pl.ds(first, width)].reshape(lanes, HEAD)
+        products = grads.astype(jnp.float32) * outs.astype(jnp.float32)
+        delta = jnp.sum(jnp.transpose(products), axis=0, keepdims=True)
+        log_row = log_ref[place][:1]
+        low, high = key_rows_of(row)
+
+        def one_row(key_row, total):
+            for block in row_blocks(width, key_row):
+                scores = nt_dot(kvq_ref[block, 0], queries) * scale
+                scores = scores + bias_ref[block, place]
+                weights = jnp.exp2(scores - log_row)
+                grad_probs = nt_dot(kvq_ref[block, 1], grads)
+                grad_scores = (weights * (grad_probs - delta)).astype(jnp.bfloat16)
+                value_acc[block] += nn_dot(weights.astype(jnp.bfloat16), grads)
+                key_acc[block] += nn_dot(grad_scores, queries)
+                total = total + nn_dot(kt_ref[block], grad_scores)
+            return total
+
+        total = lax.fori_loop(low, high, one_row, jnp.zeros((HEAD, lanes), jnp.float32))
+        terms_ref[pl.ds(first, width), 0] = (
+            (jnp.transpose(total) * factor).astype(jnp.bfloat16).reshape(width, BLOCK, HEAD)
+        )
+        return 0
+
+    lax.fori_loop(0, steps, step, 0)
+    for block in range(blocks):
+        terms_ref[block, 1] = (key_acc[block] * factor).astype(jnp.bfloat16)
+        terms_ref[block, 2] = value_acc[block].astype(jnp.bfloat16)
+
+
+def in_vmem(count):
+    return [pl.BlockSpec(memory_space=pltpu.VMEM)] * count
+
+
+def forward_head(width, kvq, bias):
+    blocks = kvq.shape[0]
+    steps, lanes = query_places(width)
+    pairs = blocks * blocks * BLOCK * BLOCK
+    return pl.pallas_call(
+        functools.partial(forward_kernel, width),
+        out_shape=(
+            jax.ShapeDtypeStruct((blocks, BLOCK, HEAD), jnp.bfloat16),
+            jax.ShapeDtypeStruct((steps, 8, lanes), jnp.float32),
+        ),
+        in_specs=in_vmem(2),
+        out_specs=tuple(in_vmem(2)),
+        scratch_shapes=[
+            pltpu.VMEM((blocks, BLOCK, lanes), jnp.float32),
+            pltpu.VMEM((blocks, HEAD, BLOCK), jnp.bfloat16),
+        ],
+        cost_estimate=pl.CostEstimate(
+            flops=4 * pairs * HEAD, bytes_accessed=4 * kvq.size, transcendentals=pairs
+        ),
+        name="forward_head",
+    )(kvq, bias)
+
+
+def backward_head(width, kvq, grads, outs, logs, bias):
+    blocks = kvq.shape[0]
+    pairs = blocks * blocks * BLOCK * BLOCK
+    return pl.pallas_call(
+        functools.partial(backward_kernel, width),
+        out_shape=jax.ShapeDtypeStruct((blocks, 3, BLOCK, HEAD), jnp.bfloat16),
+        in_specs=in_vmem(5),
+        out_specs=pl.BlockSpec(memory_space=pltpu.VMEM),
+        scratch_shapes=[
+            pltpu.VMEM((blocks, HEAD, BLOCK), jnp.bfloat16),
+            pltpu.VMEM((blocks, BLOCK, HEAD), jnp.float32),
+            pltpu.VMEM((blocks, BLOCK, HEAD), jnp.float32),
+        ],
+        cost_estimate=pl.CostEstimate(
+            flops=10 * pairs * HEAD, bytes_accessed=8 * kvq.size, transcendentals=pairs
+        ),
+        name="backward_head",
+    )(kvq, grads, outs, logs, bias)
+
+
+def mask_bias(kv_slots, blocks, width):
+    listed = jnp.any(
+        kv_slots[:, :, None] == jnp.arange(blocks, dtype=jnp.int32)[None, None, :], axis=1
+    )
+    bias = jnp.where(jnp.transpose(listed), 0.0, masked_score).astype(jnp.float32)
+    steps, lanes = query_places(width)
+    bias = jnp.broadcast_to(bias[:, :, None], (blocks, blocks, BLOCK))
+    return bias.reshape(blocks, steps, 1, lanes)
+
+
+def by_head(tensors, devices):
+    stacked = jnp.stack([tensor.reshape(BLOCK, HEADS, HEAD) for tensor in tensors])
+    stacked = jnp.transpose(stacked, (2, 0, 1, 3))
+    return jnp.pad(stacked, ((0, devices - HEADS), (0, 0), (0, 0), (0, 0)))
+
+
+def to_tokens(received):
+    return jnp.transpose(received[:HEADS], (1, 0, 2)).reshape(BLOCK, HEADS * HEAD)
+
+
+def swap(value):
+    return lax.all_to_all(value, "ctx", 0, 0, tiled=True)
+
+
+def heads_body(query, key_rows, value, grad_out, kv_slots):
+    devices = lax.axis_size("ctx")
+    width = devices // (PLANES * TILE_H)
+    bias = mask_bias(kv_slots, devices, width)
+    kvq = swap(by_head((key_rows, value, query), devices))
+    grads = swap(by_head((grad_out,), devices))[:, 0]
+    outs, logs = forward_head(width, kvq, bias)
+    out = to_tokens(swap(outs))
+    terms = swap(backward_head(width, kvq, grads, outs, logs, bias))
+    return (out, to_tokens(terms[:, 0]), to_tokens(terms[:, 1]), to_tokens(terms[:, 2]))
 
 
 def from_behind(value, axis, by):
@@ -129,7 +339,7 @@
     return (grad_keys, grad_values)
 
 
-def body(query, key_rows, value, grad_out, kv_slots):
+def neighbour_body(query, key_rows, value, grad_out, kv_slots):
     devices = lax.axis_size("ctx")
     device_index = lax.axis_index("ctx")
     row_count = query.shape[0]
@@ -218,22 +428,19 @@
 
 
 def solution(mesh):
-    placed = (
-        P(("groups", "ctx"), None),
-        P(("groups", "ctx"), None),
-        P(("groups", "ctx"), None),
-        P(("groups", "ctx"), None),
-        P(),
-    )
+    rows = P(("groups", "ctx"), None)
+    devices = mesh.shape["ctx"]
+
+    def body(query, *others):
+        one_block = query.shape[0] == BLOCK and devices % (PLANES * TILE_H) == 0
+        if one_block and HEADS <= devices <= 2 * HEADS:
+            return heads_body(query, *others)
+        return neighbour_body(query, *others)
+
     return jax.shard_map(
         body,
         mesh=mesh,
-        in_specs=placed,
-        out_specs=(
-            P(("groups", "ctx"), None),
-            P(("groups", "ctx"), None),
-            P(("groups", "ctx"), None),
-            P(("groups", "ctx"), None),
-        ),
+        in_specs=(rows, rows, rows, rows, P()),
+        out_specs=(rows, rows, rows, rows),
         check_vma=False,
     )

time: 705 us -> 144 us (0.20)
  starting transfers between devices: 382 us -> 23.5 us
  matrix products: 76.5 us -> 0 us
  local copies, waits for them, and re-layouts: 81 us -> 11 us
  waiting for transfers between devices: 137 us -> 69.8 us
  Pallas kernels: 0 us -> 37.6 us
  loops' own time: 17.8 us -> 0 us
    ppermute x78 -> x0, starting transfers between devices: 382 us -> none  [from_behind(): lax.ppermute(value, axis, [(i, (i + by) % count) for i in range(count)])]
    ppermute x78 -> x0, waiting for transfers between devices: 137 us -> none  [from_behind(): lax.ppermute(value, axis, [(i, (i + by) % count) for i in range(count)])]
    dot_general x21 -> x0, matrix products: 76.5 us -> none  [the longest x3 14.8 us: query_group(): jnp.einsum('hqk,khd->qhd', grad_scores, key_part, preferred_element_type=...]
    all_to_all x0 -> x4, waiting for transfers between devices: none -> 69.8 us  [swap(): return lax.all_to_all(value, 'ctx', 0, 0, tiled=True)]
    unnamed x91 -> x21, local copies, waits for them, and re-layouts: 55.4 us -> 6.17 us
    pallas_call x0 -> x2, Pallas kernels: none -> 37.6 us  [the longest x1 23.4 us: backward_head(): pl.pallas_call(functools.partial(backward_kernel, width), out_shape=jax.S...]
    all_to_all x0 -> x4, starting transfers between devices: none -> 23.5 us  [swap(): return lax.all_to_all(value, 'ctx', 0, 0, tiled=True)]
    another operation x3 -> x0, loops' own time: 17.8 us -> none  [the longest x1 5.95 us: body(): lax.map(lambda group_index: key_group(group_index, own_keys, own_values,...]
  transfers between devices with their start and end apart: 78 -> 4, of which waited for: 17 -> 2; matrix products, arithmetic and copies ran while one was open for 17% -> 3% of each run, Pallas kernels for 0% -> 26%
where the time goes in v1:
time: 144 us; the launch traced here: 143 us
  waiting for transfers between devices  69.8 us (48%)
  Pallas kernels  37.6 us (26%)
  starting transfers between devices  23.5 us (16%)
  local copies, waits for them, and re-layouts  11 us (8%)
    all_to_all x4, waiting for transfers between devices, swap(): return lax.all_to_all(value, 'ctx', 0, 0, tiled=True)  69.8 us
    all_to_all x4, starting transfers between devices, swap(): return lax.all_to_all(value, 'ctx', 0, 0, tiled=True)  23.5 us
    pallas_call x1, Pallas kernels, backward_head(): pl.pallas_call(functools.partial(backward_kernel, width), out_shape=jax.S...  23.4 us
    pallas_call x1, Pallas kernels, forward_head(): pl.pallas_call(functools.partial(forward_kernel, width), out_shape=(jax.S...  14.2 us
    unnamed x21, local copies, waits for them, and re-layouts  6.17 us
  transfers between devices with their start and end apart: 4, of which 2 were waited for; matrix products, arithmetic and copies ran while one was open for 3% of the time, Pallas kernels for 26%

profile of v1, /device:TPU:13, one launch (start us, length us, event | category | flops | bytes accessed | tf_op | source)
XLA Modules:
  0.0 143.2 jit_solution(16285724137235079616)
XLA Ops:
  0.6 0.0 copy-start.2
  0.6 1.3 copy.43
  1.9 0.0 copy-start.3
  1.9 0.2 copy.46
  2.2 0.0 copy-done.2
  2.2 0.2 copy.41
  2.4 0.2 copy.44
  2.6 0.3 copy-done.3
  2.9 0.2 copy.42
  3.1 0.2 copy.45
  3.4 0.1 maximum_bitcast_fusion
  3.5 1.4 pad.8
  4.9 0.0 copy-start.4
  4.9 6.7 %all-to-all-start = ((bf16[16,3,128,128]{3,2,1,0:T(8,128)(2,1)}), bf16[16,3,128,128]{3,2,1,0:T(8,128)(2,1)S(1)}, u32[]{:S(2)}, u32[]{:S(2)}) async-start(bf16[16,3,128,128]{3,2,1,0:T(8,128)(2,1)} %pad.8), calls=%async_computation | async-start | bytes 3145728 | tf_op jit(solution)/shard_map/all_to_all | solution.py:211
  11.5 0.0 copy-done.4
  11.5 0.2 copy.49
  11.8 0.2 copy.58
  12.0 0.0 copy-start.5
  12.0 0.9 pad.9.clone
  12.9 34.8 %all-to-all-done.kvq_ref = bf16[16,3,128,128]{3,2,1,0:T(8,128)(2,1)S(1)} async-done(((bf16[16,3,128,128]{3,2,1,0:T(8,128)(2,1)}), bf16[16,3,128,128]{3,2,1,0:T(8,128)(2,1)S(1)}, u32[]{:S(2)}, u32[]{:S(2)}) %all-to-all-start) | async-done | bytes 1572896 | tf_op jit(solution)/shard_map/all_to_all | solution.py:211
  47.7 0.0 copy-start
  47.7 4.8 %all-to-all-start.2 = ((bf16[16,1,128,128]{3,2,1,0:T(8,128)(2,1)}), bf16[16,1,128,128]{3,2,1,0:T(8,128)(2,1)S(1)}, u32[]{:S(2)}, u32[]{:S(2)}) async-start(bf16[16,1,128,128]{3,2,1,0:T(8,128)(2,1)} %pad.9.clone), calls=%async_computation.2 | async-start | bytes 1048576 | tf_op jit(solution)/shard_map/all_to_all | solution.py:211
  52.5 0.0 copy-done.5
  52.5 0.4 fusion
  52.9 0.1 copy.47
  52.9 0.8 broadcast_in_dim.18
  53.7 0.0 copy-done
  53.7 14.2 %forward_head.1 = (bf16[16,128,128]{2,1,0:T(8,128)(2,1)}, f32[8,8,256]{2,1,0:T(8,128)}) custom-call(bf16[16,3,128,128]{3,2,1,0:T(8,128)(2,1)} %copy-done, f32[16,8,1,256]{3,2,1,0:T(1,128)} %bitcast.39), custom_call_target="tpu_custom_call" | custom-call | flops 2147483648 | bytes 3145728 | tf_op jit(solution)/shard_map/forward_head/pallas_call | solution.py:151
  67.9 0.0 all-to-all-done.2
  67.9 0.0 copy-start.1
  67.9 6.0 %all-to-all-start.1 = ((bf16[16,128,128]{2,1,0:T(8,128)(2,1)}), bf16[16,128,128]{2,1,0:T(8,128)(2,1)S(1)}, u32[]{:S(2)}, u32[]{:S(2)}) async-start(bf16[16,128,128]{2,1,0:T(8,128)(2,1)} %get-tuple-element.6.out_ref), calls=%async_computation.1 | async-start | bytes 1048576 | tf_op jit(solution)/shard_map/all_to_all | solution.py:211
  73.9 0.0 copy-done.1
  73.9 23.4 %backward_head.1 = bf16[16,3,128,128]{3,2,1,0:T(8,128)(2,1)} custom-call(bf16[16,3,128,128]{3,2,1,0:T(8,128)(2,1)} %copy-done, bf16[16,128,128]{2,1,0:T(8,128)(2,1)} %bitcast.38, bf16[16,128,128]{2,1,0:T(8,128)(2,1)} %get-tuple-element.6.out_ref, f32[8,8,256]{2,1,0:T(8,128)} %get-tuple-element.7.log_ref, f32[16,8,1,256]{3,2,1,0:T(1,128)} %bitcast.40), custom_call_target="tpu_custom_call" | custom-call | flops 5368709120 | bytes 6291456 | tf_op jit(solution)/shard_map/backward_head/pallas_call | solution.py:173
  97.3 0.0 all-to-all-done.1
  97.3 6.0 %all-to-all-start.3 = ((bf16[16,3,128,128]{3,2,1,0:T(8,128)(2,1)}), bf16[16,3,128,128]{3,2,1,0:T(8,128)(2,1)S(1)}, u32[]{:S(2)}, u32[]{:S(2)}) async-start(bf16[16,3,128,128]{3,2,1,0:T(8,128)(2,1)} %backward_head.1), calls=%async_computation.3 | async-start | bytes 3145728 | tf_op jit(solution)/shard_map/all_to_all | solution.py:211
  103.4 0.2 copy.48
  103.6 0.9 copy.54
  104.6 35.0 %all-to-all-done.3 = bf16[16,3,128,128]{3,2,1,0:T(8,128)(2,1)S(1)} async-done(((bf16[16,3,128,128]{3,2,1,0:T(8,128)(2,1)}), bf16[16,3,128,128]{3,2,1,0:T(8,128)(2,1)S(1)}, u32[]{:S(2)}, u32[]{:S(2)}) %all-to-all-start.3) | async-done | bytes 1572896 | tf_op jit(solution)/shard_map/all_to_all | solution.py:211
  139.5 0.1 slice_bitcast_fusion
  139.7 0.2 copy.53
  139.9 0.9 copy.57
  140.8 0.2 copy.52
  141.1 0.9 copy.56
  142.0 0.2 copy.51
  142.2 0.9 copy.55
  (2 shorter events, 0.0 us)
Async XLA Ops:
  0.6 1.5 %copy-start.2 = (bf16[128,1536]{1,0:T(8,128)(2,1)S(1)}, bf16[128,1536]{1,0:T(8,128)(2,1)}, u32[]{:S(2)}) copy-start(bf16[128,1536]{1,0:T(8,128)(2,1)} %param.6) | copy-start | bytes 1179652
  1.9 1.0 copy-start.3
  4.9 6.7 %copy-start.4 = (bf16[128,1536]{1,0:T(8,128)(2,1)S(1)}, bf16[128,1536]{1,0:T(8,128)(2,1)}, u32[]{:S(2)}) copy-start(bf16[128,1536]{1,0:T(8,128)(2,1)} %param.8) | copy-start | bytes 1179652
  4.9 42.8 %all-to-all-start = ((bf16[16,3,128,128]{3,2,1,0:T(8,128)(2,1)}), bf16[16,3,128,128]{3,2,1,0:T(8,128)(2,1)S(1)}, u32[]{:S(2)}, u32[]{:S(2)}) async-start(bf16[16,3,128,128]{3,2,1,0:T(8,128)(2,1)} %pad.8), calls=%async_computation | async-start | bytes 3145728 | tf_op jit(solution)/shard_map/all_to_all | solution.py:211
  12.0 40.5 %copy-start.5 = (s32[16,18]{1,0:T(8,128)S(1)}, s32[16,18]{1,0:T(8,128)}, u32[]{:S(2)}) copy-start(s32[16,18]{1,0:T(8,128)} %param.9) | copy-start | bytes 3460
  47.7 6.0 %copy-start = (bf16[16,3,128,128]{3,2,1,0:T(8,128)(2,1)}, bf16[16,3,128,128]{3,2,1,0:T(8,128)(2,1)S(1)}, u32[]{:S(2)}) copy-start(bf16[16,3,128,128]{3,2,1,0:T(8,128)(2,1)S(1)} %all-to-all-done.kvq_ref) | copy-start | bytes 4718596
  47.7 20.2 %all-to-all-start.2 = ((bf16[16,1,128,128]{3,2,1,0:T(8,128)(2,1)}), bf16[16,1,128,128]{3,2,1,0:T(8,128)(2,1)S(1)}, u32[]{:S(2)}, u32[]{:S(2)}) async-start(bf16[16,1,128,128]{3,2,1,0:T(8,128)(2,1)} %pad.9.clone), calls=%async_computation.2 | async-start | bytes 1048576 | tf_op jit(solution)/shard_map/all_to_all | solution.py:211
  67.9 6.0 %copy-start.1 = (bf16[16,1,128,128]{3,2,1,0:T(8,128)(2,1)}, bf16[16,1,128,128]{3,2,1,0:T(8,128)(2,1)S(1)}, u32[]{:S(2)}) copy-start(bf16[16,1,128,128]{3,2,1,0:T(8,128)(2,1)S(1)} %all-to-all-done.2) | copy-start | bytes 1572868
  67.9 29.4 %all-to-all-start.1 = ((bf16[16,128,128]{2,1,0:T(8,128)(2,1)}), bf16[16,128,128]{2,1,0:T(8,128)(2,1)S(1)}, u32[]{:S(2)}, u32[]{:S(2)}) async-start(bf16[16,128,128]{2,1,0:T(8,128)(2,1)} %get-tuple-element.6.out_ref), calls=%async_computation.1 | async-start | bytes 1048576 | tf_op jit(solution)/shard_map/all_to_all | solution.py:211
  97.3 42.2 %all-to-all-start.3 = ((bf16[16,3,128,128]{3,2,1,0:T(8,128)(2,1)}), bf16[16,3,128,128]{3,2,1,0:T(8,128)(2,1)S(1)}, u32[]{:S(2)}, u32[]{:S(2)}) async-start(bf16[16,3,128,128]{3,2,1,0:T(8,128)(2,1)} %backward_head.1), calls=%async_computation.3 | async-start | bytes 3145728 | tf_op jit(solution)/shard_map/all_to_all | solution.py:211
